TPU v7x, 256 devices: a whole 4x4x8 slice. The times are simulated.
256 devices in a mesh: row: 16 (over z, core), col: 16 (over x, y).
Axes of the slice: x: 4, y: 4, z: 8, core: 2. Of those that a mesh axis runs over, the one named last changes fastest.
Arguments:
- token_ids: int32 [32, 256], P('row'), may hold values from 0 to 16383
- passage_lengths: int32 [32], P('row'), may hold values from 64 to 256, as said below
- embedding: bfloat16 [16384, 4096], P(None, 'col'), may hold values from -8 to 8
- attn_gain: bfloat16 [4096], P('col'), may hold values from 0.25 to 1.75
- final_gain: bfloat16 [4096], P('col'), may hold values from 0.25 to 1.75
- query_weight: bfloat16 [4096, 4096], P('row', 'col'), may hold values from -0.5 to 0.5
- key_weight: bfloat16 [4096, 4096], P('row', 'col'), may hold values from -0.5 to 0.5
- value_weight: bfloat16 [4096, 4096], P('row', 'col'), may hold values from -0.09375 to 0.09375
- out_weight: bfloat16 [4096, 4096], P('row', 'col'), may hold values from -0.09375 to 0.09375
- crosskey_weight: bfloat16 [4096, 4096], P('row', 'col'), may hold values from -0.09375 to 0.09375
- crossvalue_weight: bfloat16 [4096, 4096], P('row', 'col'), may hold values from -0.09375 to 0.09375
Outputs:
- hidden_out: bfloat16 [8192, 4096], P('row', 'col')
- cross_keys: bfloat16 [8192, 16, 256], P('row', 'col')
- cross_values: bfloat16 [8192, 16, 256], P('row', 'col')
Inputs may be any that keep to these rules, and one draw needn't show every extreme that they name: `passage_lengths`: some passage of every draw has all 256 slots valid.
All inputs are finite; a program needn't handle non-finite values.
Results may differ from a plain program's by a relative error of at most 0.0082.
Values may be sent and summed in bfloat16 or wider, within the bound.
No kernel may reach another device: no remote copies, remote signals or barrier semaphores. Data moves between devices by JAX's collectives and lax.ppermute only.
A program may use at most 64 MiB of HBM per device.

v0:
```python
import jax
import jax.numpy as jnp
from jax import lax
from jax.sharding import PartitionSpec as P

D = 4096
HD = 256
PLEN = 256
epsilon = 1e-06
masked_score = -1000000000.0


def scaled_rows(widened, summed, gain_row):
    inverse = lax.rsqrt(summed / D + epsilon)
    return (widened * inverse * gain_row.astype(jnp.float32)).astype(jnp.bfloat16)


def spread_norm(row_block, gain_row, which):
    widened = row_block.astype(jnp.float32)
    partial_sum = jnp.sum(widened * widened, axis=1, keepdims=True)
    if which == 0:
        summed = lax.psum(partial_sum, "col")
        return lax.all_gather(
            scaled_rows(widened, summed, gain_row[None, :]), "col", axis=1, tiled=True
        )
    else:
        summed = lax.psum(partial_sum, "col")
        return lax.all_gather(
            scaled_rows(widened, summed, gain_row[None, :]), "col", axis=1, tiled=True
        )


def add_terms(source, pieces):
    return tuple(
        (
            jnp.dot(source, weight_piece, preferred_element_type=jnp.float32)
            for weight_piece in pieces
        )
    )


def attend(query_rows, key_rows, value_rows, passage_lengths):
    tok_rows, local_width = query_rows.shape
    passages_here = tok_rows // PLEN
    heads_here = local_width // HD
    query_four = query_rows.reshape(passages_here, PLEN, heads_here, HD)
    key_four = key_rows.reshape(passages_here, PLEN, heads_here, HD)
    value_four = value_rows.reshape(passages_here, PLEN, heads_here, HD)
    scores = jnp.einsum(
        "pihd,pjhd->phij", query_four, key_four, preferred_element_type=jnp.float32
    ) * HD ** (-0.5)
    valid = jnp.arange(PLEN, dtype=jnp.int32)[None, :] < passage_lengths[:, None]
    scores = jnp.where(valid[:, None, None, :], scores, masked_score)
    highest = jnp.max(scores, axis=-1, keepdims=True)
    expon = jnp.exp(scores - highest)
    probs = (expon / jnp.sum(expon, axis=-1, keepdims=True)).astype(jnp.bfloat16)
    mixed = jnp.einsum("phij,pjhd->pihd", probs, value_four, preferred_element_type=jnp.float32)
    return mixed.astype(jnp.bfloat16).reshape(tok_rows, local_width)


def shards(
    token_ids,
    passage_lengths,
    embedding,
    attn_gain,
    final_gain,
    query_weight,
    key_weight,
    value_weight,
    out_weight,
    crosskey_weight,
    crossvalue_weight,
):
    embedded = jnp.take(embedding, token_ids.reshape(-1), axis=0)
    normed = spread_norm(embedded, attn_gain, 0)
    tok_rows = normed.shape[0]
    local_width = query_weight.shape[1]
    query_sum, key_sum, value_sum = add_terms(
        normed,
        (
            lax.all_gather(query_weight, "row", axis=0, tiled=True),
            lax.all_gather(key_weight, "row", axis=0, tiled=True),
            lax.all_gather(value_weight, "row", axis=0, tiled=True),
        ),
    )
    attended = attend(
        query_sum.astype(jnp.bfloat16),
        key_sum.astype(jnp.bfloat16),
        value_sum.astype(jnp.bfloat16),
        passage_lengths,
    )
    heads_full = lax.all_gather(attended, "col", axis=1, tiled=True)
    (projected,) = add_terms(heads_full, (lax.all_gather(out_weight, "row", axis=0, tiled=True),))
    hidden_out = (embedded.astype(jnp.float32) + projected).astype(jnp.bfloat16)
    final_normed = spread_norm(hidden_out, final_gain, 1)
    crosskey_sum, crossvalue_sum = add_terms(
        final_normed,
        (
            lax.all_gather(crosskey_weight, "row", axis=0, tiled=True),
            lax.all_gather(crossvalue_weight, "row", axis=0, tiled=True),
        ),
    )
    heads_here = local_width // HD
    cross_keys = crosskey_sum.astype(jnp.bfloat16).reshape(tok_rows, heads_here, HD)
    cross_values = crossvalue_sum.astype(jnp.bfloat16).reshape(tok_rows, heads_here, HD)
    return (hidden_out, cross_keys, cross_values)


def solution(mesh):
    return jax.shard_map(
        shards,
        mesh=mesh,
        in_specs=(
            P("row", None),
            P("row"),
            P(None, "col"),
            P("col"),
            P("col"),
            P("row", "col"),
            P("row", "col"),
            P("row", "col"),
            P("row", "col"),
            P("row", "col"),
            P("row", "col"),
        ),
        out_specs=(P("row", "col"), P("row", "col", None), P("row", "col", None)),
        check_vma=False,
    )
```

profile of v0, /device:TPU:1, one launch (start us, length us, event | category | flops | bytes accessed | tf_op | source)
XLA Modules:
  0.0 447.0 jit_solution(17359749313425114075)
XLA Ops:
  7.2 0.0 copy-start
  7.2 0.0 all-gather.14.cloned.1.call-start
  7.2 0.7 all-gather.14.cloned.1.call-update
  7.9 0.0 all-gather.10.cloned.1.call-start
  8.0 0.7 convert_element_type.53
  8.6 0.7 copy.22
  9.3 0.0 copy-start.1
  9.3 6.0 %gather_fusion = bf16[512,256]{1,0:T(8,128)(2,1)S(1)} fusion(bf16[16384,256]{1,0:T(8,128)(2,1)} %param.13, s32[1024]{0:T(1024)S(1)} %pad_clamp_fusion), kind=kCustom, calls=%fused_computation | custom fusion | bytes 526336 | tf_op jit(solution)/shard_map/jit(_take)/gather | solution.py:74
  15.4 0.1 copy.17
  15.5 0.0 copy-done
  15.5 0.1 fusion.10
  15.6 34.2 %psum.14 = f32[512,1]{0,1:T(1,128)S(1)} all-reduce(f32[512,1]{0,1:T(1,128)S(1)} %bitcast.48), channel_id=1, replica_groups=mesh['row'=16,'col'=16] {'col'}, use_global_device_ids=true, to_apply=%region_1.2 | all-reduce | flops 512 | bytes 4096 | tf_op jit(solution)/shard_map/psum | solution.py:22
  49.9 0.8 fusion.12
  50.7 0.0 all-gather.10.cloned.1.call-update
  50.7 0.0 all-gather.16.cloned.1.call-start
  50.8 0.7 all-gather.16.cloned.1.call-update
  51.5 0.0 all-gather.12.cloned.1.call-start
  51.5 0.5 all-gather.12.cloned.1.call-update
  52.0 0.0 all-gather.20.cloned.1.call-start
  52.1 0.5 all-gather.20.cloned.1.call-update
  52.6 0.0 all-gather.18.cloned.1.call-start
  52.7 0.0 copy-done.1
  52.7 0.1 iota_compare_fusion
  52.8 0.7 all-gather.14.cloned.1.call-done
  53.5 58.8 %all-gather.10.cloned.1.call-done = bf16[512,4096]{0,1:T(8,128)(2,1)} async-done(((bf16[512,256]{0,1:T(8,128)(2,1)}), bf16[512,4096]{0,1:T(8,128)(2,1)}) %all-gather.10.cloned.1.call-update) | async-done | bytes 4194320 | tf_op jit(solution)/shard_map/all_gather | solution.py:23
  112.3 4.2 convolution_convert_fusion.4
  116.4 37.4 %all-gather.16.cloned.1.call-done = bf16[4096,256]{1,0:T(8,128)(2,1)} async-done(((bf16[256,256]{1,0:T(8,128)(2,1)}), bf16[4096,256]{1,0:T(8,128)(2,1)}) %all-gather.16.cloned.1.call-update) | async-done | bytes 2097168 | tf_op jit(solution)/shard_map/all_gather | solution.py:82
  153.9 4.2 convolution_convert_fusion.3
  158.0 0.4 fusion.15
  158.4 0.3 fusion.3
  158.7 34.7 %all-gather.12.cloned.1.call-done = bf16[4096,256]{1,0:T(8,128)(2,1)} async-done(((bf16[256,256]{1,0:T(8,128)(2,1)}), bf16[4096,256]{1,0:T(8,128)(2,1)}) %all-gather.12.cloned.1.call-update) | async-done | bytes 2097168 | tf_op jit(solution)/shard_map/all_gather | solution.py:83
  193.4 4.2 convolution_convert_fusion.5
  197.6 0.0 copy-start.2
  197.6 1.0 convolution_convert_fusion.2
  198.6 0.0 all-gather.18.cloned.1.call-update
  198.6 0.0 all-gather.24.cloned.1.call-start
  198.7 0.7 all-gather.24.cloned.1.call-update
  199.4 0.0 all-gather.22.cloned.1.call-start
  199.4 0.0 copy-done.2
  199.5 33.5 %all-gather.20.cloned.1.call-done = bf16[4096,256]{1,0:T(8,128)(2,1)} async-done(((bf16[256,256]{1,0:T(8,128)(2,1)}), bf16[4096,256]{1,0:T(8,128)(2,1)}) %all-gather.20.cloned.1.call-update) | async-done | bytes 2097168 | tf_op jit(solution)/shard_map/all_gather | solution.py:93
  232.9 61.3 %all-gather.18.cloned.1.call-done = bf16[512,4096]{1,0:T(8,128)(2,1)} async-done(((bf16[512,256]{1,0:T(8,128)(2,1)}), bf16[512,4096]{1,0:T(8,128)(2,1)}) %all-gather.18.cloned.1.call-update) | async-done | bytes 4194320 | tf_op jit(solution)/shard_map/all_gather | solution.py:92
  294.2 4.2 fusion.7
  298.4 31.3 %psum.15 = f32[512,1]{0,1:T(1,128)S(1)} all-reduce(f32[512,1]{0,1:T(1,128)S(1)} %bitcast.54), channel_id=1, replica_groups=mesh['row'=16,'col'=16] {'col'}, use_global_device_ids=true, to_apply=%region_5.6 | all-reduce | flops 512 | bytes 4096 | tf_op jit(solution)/shard_map/psum | solution.py:27
  329.7 0.8 fusion.9
  330.5 0.0 all-gather.22.cloned.1.call-update
  330.5 0.0 all-gather.26.cloned.1.call-start
  330.6 0.7 all-gather.26.cloned.1.call-update
  331.3 0.8 copy.19
  332.1 4.6 %all-gather.24.cloned.1.call-done = bf16[4096,256]{1,0:T(8,128)(2,1)} async-done(((bf16[256,256]{1,0:T(8,128)(2,1)}), bf16[4096,256]{1,0:T(8,128)(2,1)}) %all-gather.24.cloned.1.call-update) | async-done | bytes 2097168 | tf_op jit(solution)/shard_map/all_gather | solution.py:99
  336.7 57.3 %all-gather.22.cloned.1.call-done = bf16[512,4096]{0,1:T(8,128)(2,1)} async-done(((bf16[512,256]{0,1:T(8,128)(2,1)}), bf16[512,4096]{0,1:T(8,128)(2,1)}) %all-gather.22.cloned.1.call-update) | async-done | bytes 4194320 | tf_op jit(solution)/shard_map/all_gather | solution.py:28
  394.0 4.9 %fusion.5 = bf16[512,1,256]{2,0,1:T(8,128)(2,1)} fusion(bf16[512,4096]{0,1:T(8,128)(2,1)} %all-gather.22.cloned.1.call-done, bf16[4096,256]{1,0:T(8,128)(2,1)} %all-gather.24.cloned.1.call-done), kind=kOutput, calls=%fused_computation.14 | convolution fusion | flops 1073872896 | bytes 6553600 | tf_op jit(solution)/shard_map/dot_general | solution.py:36
  398.8 36.7 %all-gather.26.cloned.1.call-done = bf16[4096,256]{1,0:T(8,128)(2,1)} async-done(((bf16[256,256]{1,0:T(8,128)(2,1)}), bf16[4096,256]{1,0:T(8,128)(2,1)}) %all-gather.26.cloned.1.call-update) | async-done | bytes 2097168 | tf_op jit(solution)/shard_map/all_gather | solution.py:100
  435.6 4.9 %fusion.6 = bf16[512,1,256]{2,0,1:T(8,128)(2,1)} fusion(bf16[512,4096]{0,1:T(8,128)(2,1)} %all-gather.22.cloned.1.call-done, bf16[4096,256]{1,0:T(8,128)(2,1)} %all-gather.26.cloned.1.call-done), kind=kOutput, calls=%fused_computation.15 | convolution fusion | flops 1073872896 | bytes 6553600 | tf_op jit(solution)/shard_map/dot_general | solution.py:36
  (7 shorter events, 0.1 us)
Async XLA Ops:
  7.2 8.3 %copy-start = (s32[2,256]{1,0:T(2,128)S(1)}, s32[2,256]{1,0:T(2,128)}, u32[]{:S(2)}) copy-start(s32[2,256]{1,0:T(2,128)} %param.11) | copy-start | bytes 6148
  7.2 46.3 %all-gather.14.cloned.1.call-start = ((), (), s32[]{:S(2)}) async-start(), calls=%async_computation.2 | async-start | bytes 2228224 | tf_op jit(solution)/shard_map/all_gather | solution.py:81
  7.9 104.3 %all-gather.10.cloned.1.call-start = ((), (), s32[]{:S(2)}) async-start(), calls=%async_computation | async-start | bytes 4456448 | tf_op jit(solution)/shard_map/all_gather | solution.py:23
  9.3 43.4 %copy-start.1 = (s32[2]{0:T(128)S(1)}, s32[2]{0:T(128)}, u32[]{:S(2)}) copy-start(s32[2]{0:T(128)} %param.12) | copy-start | bytes 28
  50.7 103.1 %all-gather.16.cloned.1.call-start = ((), (), s32[]{:S(2)}) async-start(), calls=%async_computation.3 | async-start | bytes 2228224 | tf_op jit(solution)/shard_map/all_gather | solution.py:82
  51.5 141.9 %all-gather.12.cloned.1.call-start = ((), (), s32[]{:S(2)}) async-start(), calls=%async_computation.1 | async-start | bytes 2228224 | tf_op jit(solution)/shard_map/all_gather | solution.py:83
  52.0 180.9 %all-gather.20.cloned.1.call-start = ((), (), s32[]{:S(2)}) async-start(), calls=%async_computation.5 | async-start | bytes 2228224 | tf_op jit(solution)/shard_map/all_gather | solution.py:93
  52.6 241.6 %all-gather.18.cloned.1.call-start = ((), (), s32[]{:S(2)}) async-start(), calls=%async_computation.4 | async-start | bytes 4456448 | tf_op jit(solution)/shard_map/all_gather | solution.py:92
  197.6 1.9 copy-start.2
  198.6 138.1 %all-gather.24.cloned.1.call-start = ((), (), s32[]{:S(2)}) async-start(), calls=%async_computation.7 | async-start | bytes 2228224 | tf_op jit(solution)/shard_map/all_gather | solution.py:99
  199.4 194.6 %all-gather.22.cloned.1.call-start = ((), (), s32[]{:S(2)}) async-start(), calls=%async_computation.6 | async-start | bytes 4456448 | tf_op jit(solution)/shard_map/all_gather | solution.py:28
  330.5 105.1 %all-gather.26.cloned.1.call-start = ((), (), s32[]{:S(2)}) async-start(), calls=%async_computation.8 | async-start | bytes 2228224 | tf_op jit(solution)/shard_map/all_gather | solution.py:100
Sparse Core Ops, SparseCore 0:
  9.8 43.6 all-gather.13
  56.5 55.7 all-gather.9
  114.1 39.7 all-gather.15
  155.5 37.8 all-gather.11
  195.1 37.8 all-gather.19
  235.7 58.4 all-gather.17
  296.0 40.6 all-gather.23
  339.7 54.2 all-gather.21
  395.8 39.7 all-gather.25
where the time goes:
time: 447 us
  waiting for transfers between devices  329 us (74%)
  blocking collectives  65.5 us (15%)
  matrix products  28.1 us (6%)
  between operations  14 us (3%)
  local copies, waits for them, and re-layouts  7.71 us (2%)
    all_gather x2, waiting for transfers between devices, spread_norm(): lax.all_gather(scaled_rows(widened, summed, gain_row[None, :]), 'col', ax...  116 us
    psum x2, blocking collectives, spread_norm(): summed = lax.psum(partial_sum, 'col')  65.5 us
    all_gather x1, waiting for transfers between devices, shards(): heads_full = lax.all_gather(attended, 'col', axis=1, tiled=True)  61.3 us
    all_gather x1, waiting for transfers between devices, shards(): lax.all_gather(key_weight, 'row', axis=0, tiled=True)  37.4 us
    all_gather x1, waiting for transfers between devices, shards(): lax.all_gather(crossvalue_weight, 'row', axis=0, tiled=True)  36.7 us
    all_gather x1, waiting for transfers between devices, shards(): lax.all_gather(value_weight, 'row', axis=0, tiled=True)  34.7 us
    all_gather x1, waiting for transfers between devices, shards(): lax.all_gather(out_weight, 'row', axis=0, tiled=True)  33.5 us
    dot_general x6, matrix products, add_terms(): jnp.dot(source, weight_piece, preferred_element_type=jnp.float32)  26.4 us
  transfers between devices with their start and end apart: 9, of which 9 were waited for; matrix products, arithmetic and copies ran while one was open for 7% of the time, Pallas kernels for 0%

commit v1 on v0

--- a/solution.py
+++ b/solution.py
@@ -19,7 +19,7 @@
     widened = row_block.astype(jnp.float32)
     partial_sum = jnp.sum(widened * widened, axis=1, keepdims=True)
     if which == 0:
-        summed = lax.psum(partial_sum, "col")
+        summed = jnp.sum(lax.all_gather(partial_sum, "col"), axis=0)
         return lax.all_gather(
             scaled_rows(widened, summed, gain_row[None, :]), "col", axis=1, tiled=True
         )

time: 447 us -> 446 us (level)
  blocking collectives: 65.5 us -> 51.1 us
  waiting for transfers between devices: 329 us -> 342 us
    psum x2 -> x1, blocking collectives: 65.5 us -> 31.3 us  [spread_norm(): summed = lax.psum(partial_sum, 'col')]
    all_gather x0 -> x1, blocking collectives: none -> 19.8 us  [spread_norm(): summed = jnp.sum(lax.all_gather(partial_sum, 'col'), axis=0)]
    all_gather x1, waiting for transfers between devices: 0.71 us -> 15.1 us  [shards(): lax.all_gather(query_weight, 'row', axis=0, tiled=True)]
  transfers between devices with their start and end apart: 9 -> 9, of which waited for: 9 -> 9; matrix products, arithmetic and copies ran while one was open for 7% -> 8% of each run, Pallas kernels for 0% -> 0%
where the time goes in v1:
time: 446 us; the launch traced here: 445 us
  waiting for transfers between devices  342 us (77%)
  blocking collectives  51.1 us (11%)
  matrix products  28.1 us (6%)
  between operations  14 us (3%)
  local copies, waits for them, and re-layouts  7.71 us (2%)
    all_gather x2, waiting for transfers between devices, spread_norm(): lax.all_gather(scaled_rows(widened, summed, gain_row[None, :]), 'col', ax...  115 us
    all_gather x1, waiting for transfers between devices, shards(): heads_full = lax.all_gather(attended, 'col', axis=1, tiled=True)  61.3 us
    all_gather x1, waiting for transfers between devices, shards(): lax.all_gather(key_weight, 'row', axis=0, tiled=True)  37.4 us
    all_gather x1, waiting for transfers between devices, shards(): lax.all_gather(crossvalue_weight, 'row', axis=0, tiled=True)  36.7 us
    all_gather x1, waiting for transfers between devices, shards(): lax.all_gather(value_weight, 'row', axis=0, tiled=True)  34.7 us
    all_gather x1, waiting for transfers between devices, shards(): lax.all_gather(out_weight, 'row', axis=0, tiled=True)  33.5 us
    psum x1, blocking collectives, spread_norm(): summed = lax.psum(partial_sum, 'col')  31.3 us
    dot_general x6, matrix products, add_terms(): jnp.dot(source, weight_piece, preferred_element_type=jnp.float32)  26.4 us
  transfers between devices with their start and end apart: 9, of which 9 were waited for; matrix products, arithmetic and copies ran while one was open for 8% of the time, Pallas kernels for 0%

profile of v1, /device:TPU:1, one launch (start us, length us, event | category | flops | bytes accessed | tf_op | source)
XLA Modules:
  0.0 445.5 jit_solution(10929252409085733325)
XLA Ops:
  7.2 0.0 copy-start
  7.2 0.0 all-gather.16.cloned.1.call-start
  7.2 0.7 all-gather.16.cloned.1.call-update
  7.9 0.0 all-gather.12.cloned.1.call-start
  8.0 0.7 convert_element_type.53
  8.6 0.7 copy.25
  9.3 0.0 copy-start.1
  9.3 6.0 %gather_fusion = bf16[512,256]{1,0:T(8,128)(2,1)S(1)} fusion(bf16[16384,256]{1,0:T(8,128)(2,1)} %param.13, s32[1024]{0:T(1024)S(1)} %pad_clamp_fusion), kind=kCustom, calls=%fused_computation | custom fusion | bytes 526336 | tf_op jit(solution)/shard_map/jit(_take)/gather | solution.py:74
  15.4 0.1 copy.20
  15.5 0.0 copy-done
  15.5 0.1 fusion.10
  15.6 19.8 %all-gather.1 = f32[16,1,512]{2,1,0:T(1,128)S(1)} all-gather(f32[1,1,512]{2,1,0:T(1,128)S(1)} %bitcast.45), channel_id=2, replica_groups=mesh['row'=16,'col'=16] {'col'}, dimensions={0}, use_global_device_ids=true | all-gather | bytes 34816 | tf_op jit(solution)/shard_map/all_gather | solution.py:22
  35.5 0.8 fusion.12
  36.3 0.0 all-gather.12.cloned.1.call-update
  36.3 0.0 all-gather.18.cloned.1.call-start
  36.4 0.7 all-gather.18.cloned.1.call-update
  37.1 0.0 all-gather.14.cloned.1.call-start
  37.1 0.5 all-gather.14.cloned.1.call-update
  37.6 0.0 all-gather.22.cloned.1.call-start
  37.7 0.5 all-gather.22.cloned.1.call-update
  38.2 0.0 all-gather.20.cloned.1.call-start
  38.3 0.0 copy-done.1
  38.3 0.1 iota_compare_fusion
  38.4 15.1 %all-gather.16.cloned.1.call-done = bf16[4096,256]{1,0:T(8,128)(2,1)} async-done(((bf16[256,256]{1,0:T(8,128)(2,1)}), bf16[4096,256]{1,0:T(8,128)(2,1)}) %all-gather.16.cloned.1.call-update) | async-done | bytes 2097168 | tf_op jit(solution)/shard_map/all_gather | solution.py:81
  53.5 57.3 %all-gather.12.cloned.1.call-done = bf16[512,4096]{0,1:T(8,128)(2,1)} async-done(((bf16[512,256]{0,1:T(8,128)(2,1)}), bf16[512,4096]{0,1:T(8,128)(2,1)}) %all-gather.12.cloned.1.call-update) | async-done | bytes 4194320 | tf_op jit(solution)/shard_map/all_gather | solution.py:23
  110.7 4.2 convolution_convert_fusion.4
  114.9 37.4 %all-gather.18.cloned.1.call-done = bf16[4096,256]{1,0:T(8,128)(2,1)} async-done(((bf16[256,256]{1,0:T(8,128)(2,1)}), bf16[4096,256]{1,0:T(8,128)(2,1)}) %all-gather.18.cloned.1.call-update) | async-done | bytes 2097168 | tf_op jit(solution)/shard_map/all_gather | solution.py:82
  152.4 4.2 convolution_convert_fusion.3
  156.5 0.4 fusion.15
  156.9 0.3 fusion.3
  157.2 34.7 %all-gather.14.cloned.1.call-done = bf16[4096,256]{1,0:T(8,128)(2,1)} async-done(((bf16[256,256]{1,0:T(8,128)(2,1)}), bf16[4096,256]{1,0:T(8,128)(2,1)}) %all-gather.14.cloned.1.call-update) | async-done | bytes 2097168 | tf_op jit(solution)/shard_map/all_gather | solution.py:83
  191.9 4.2 convolution_convert_fusion.5
  196.1 0.0 copy-start.2
  196.1 1.0 convolution_convert_fusion.2
  197.1 0.0 all-gather.20.cloned.1.call-update
  197.1 0.0 all-gather.26.cloned.1.call-start
  197.2 0.7 all-gather.26.cloned.1.call-update
  197.9 0.0 all-gather.24.cloned.1.call-start
  197.9 0.0 copy-done.2
  197.9 33.5 %all-gather.22.cloned.1.call-done = bf16[4096,256]{1,0:T(8,128)(2,1)} async-done(((bf16[256,256]{1,0:T(8,128)(2,1)}), bf16[4096,256]{1,0:T(8,128)(2,1)}) %all-gather.22.cloned.1.call-update) | async-done | bytes 2097168 | tf_op jit(solution)/shard_map/all_gather | solution.py:93
  231.4 61.3 %all-gather.20.cloned.1.call-done = bf16[512,4096]{1,0:T(8,128)(2,1)} async-done(((bf16[512,256]{1,0:T(8,128)(2,1)}), bf16[512,4096]{1,0:T(8,128)(2,1)}) %all-gather.20.cloned.1.call-update) | async-done | bytes 4194320 | tf_op jit(solution)/shard_map/all_gather | solution.py:92
  292.7 4.2 fusion.7
  296.9 31.3 %psum.7 = f32[512,1]{0,1:T(1,128)S(1)} all-reduce(f32[512,1]{0,1:T(1,128)S(1)} %bitcast.52), channel_id=1, replica_groups=mesh['row'=16,'col'=16] {'col'}, use_global_device_ids=true, to_apply=%region_5.6 | all-reduce | flops 512 | bytes 4096 | tf_op jit(solution)/shard_map/psum | solution.py:27
  328.2 0.8 fusion.9
  329.0 0.0 all-gather.24.cloned.1.call-update
  329.0 0.0 all-gather.28.cloned.1.call-start
  329.1 0.7 all-gather.28.cloned.1.call-update
  329.8 0.8 copy.22
  330.6 4.6 %all-gather.26.cloned.1.call-done = bf16[4096,256]{1,0:T(8,128)(2,1)} async-done(((bf16[256,256]{1,0:T(8,128)(2,1)}), bf16[4096,256]{1,0:T(8,128)(2,1)}) %all-gather.26.cloned.1.call-update) | async-done | bytes 2097168 | tf_op jit(solution)/shard_map/all_gather | solution.py:99
  335.2 57.3 %all-gather.24.cloned.1.call-done = bf16[512,4096]{0,1:T(8,128)(2,1)} async-done(((bf16[512,256]{0,1:T(8,128)(2,1)}), bf16[512,4096]{0,1:T(8,128)(2,1)}) %all-gather.24.cloned.1.call-update) | async-done | bytes 4194320 | tf_op jit(solution)/shard_map/all_gather | solution.py:28
  392.5 4.9 %fusion.5 = bf16[512,1,256]{2,0,1:T(8,128)(2,1)} fusion(bf16[512,4096]{0,1:T(8,128)(2,1)} %all-gather.24.cloned.1.call-done, bf16[4096,256]{1,0:T(8,128)(2,1)} %all-gather.26.cloned.1.call-done), kind=kOutput, calls=%fused_computation.14 | convolution fusion | flops 1073872896 | bytes 6553600 | tf_op jit(solution)/shard_map/dot_general | solution.py:36
  397.3 36.7 %all-gather.28.cloned.1.call-done = bf16[4096,256]{1,0:T(8,128)(2,1)} async-done(((bf16[256,256]{1,0:T(8,128)(2,1)}), bf16[4096,256]{1,0:T(8,128)(2,1)}) %all-gather.28.cloned.1.call-update) | async-done | bytes 2097168 | tf_op jit(solution)/shard_map/all_gather | solution.py:100
  434.1 4.9 %fusion.6 = bf16[512,1,256]{2,0,1:T(8,128)(2,1)} fusion(bf16[512,4096]{0,1:T(8,128)(2,1)} %all-gather.24.cloned.1.call-done, bf16[4096,256]{1,0:T(8,128)(2,1)} %all-gather.28.cloned.1.call-done), kind=kOutput, calls=%fused_computation.15 | convolution fusion | flops 1073872896 | bytes 6553600 | tf_op jit(solution)/shard_map/dot_general | solution.py:36
  (8 shorter events, 0.1 us)
Async XLA Ops:
  7.2 8.3 %copy-start = (s32[2,256]{1,0:T(2,128)S(1)}, s32[2,256]{1,0:T(2,128)}, u32[]{:S(2)}) copy-start(s32[2,256]{1,0:T(2,128)} %param.11) | copy-start | bytes 6148
  7.2 46.3 %all-gather.16.cloned.1.call-start = ((), (), s32[]{:S(2)}) async-start(), calls=%async_computation.2 | async-start | bytes 2228224 | tf_op jit(solution)/shard_map/all_gather | solution.py:81
  7.9 102.8 %all-gather.12.cloned.1.call-start = ((), (), s32[]{:S(2)}) async-start(), calls=%async_computation | async-start | bytes 4456448 | tf_op jit(solution)/shard_map/all_gather | solution.py:23
  9.3 29.0 %copy-start.1 = (s32[2]{0:T(128)S(1)}, s32[2]{0:T(128)}, u32[]{:S(2)}) copy-start(s32[2]{0:T(128)} %param.12) | copy-start | bytes 28
  36.3 116.0 %all-gather.18.cloned.1.call-start = ((), (), s32[]{:S(2)}) async-start(), calls=%async_computation.3 | async-start | bytes 2228224 | tf_op jit(solution)/shard_map/all_gather | solution.py:82
  37.1 154.8 %all-gather.14.cloned.1.call-start = ((), (), s32[]{:S(2)}) async-start(), calls=%async_computation.1 | async-start | bytes 2228224 | tf_op jit(solution)/shard_map/all_gather | solution.py:83
  37.6 193.8 %all-gather.22.cloned.1.call-start = ((), (), s32[]{:S(2)}) async-start(), calls=%async_computation.5 | async-start | bytes 2228224 | tf_op jit(solution)/shard_map/all_gather | solution.py:93
  38.2 254.5 %all-gather.20.cloned.1.call-start = ((), (), s32[]{:S(2)}) async-start(), calls=%async_computation.4 | async-start | bytes 4456448 | tf_op jit(solution)/shard_map/all_gather | solution.py:92
  196.1 1.9 copy-start.2
  197.1 138.1 %all-gather.26.cloned.1.call-start = ((), (), s32[]{:S(2)}) async-start(), calls=%async_computation.7 | async-start | bytes 2228224 | tf_op jit(solution)/shard_map/all_gather | solution.py:99
  197.9 194.6 %all-gather.24.cloned.1.call-start = ((), (), s32[]{:S(2)}) async-start(), calls=%async_computation.6 | async-start | bytes 4456448 | tf_op jit(solution)/shard_map/all_gather | solution.py:28
  329.0 105.1 %all-gather.28.cloned.1.call-start = ((), (), s32[]{:S(2)}) async-start(), calls=%async_computation.8 | async-start | bytes 2228224 | tf_op jit(solution)/shard_map/all_gather | solution.py:100
Sparse Core Ops, SparseCore 0:
  9.8 43.6 all-gather.15
  56.5 54.2 all-gather.11
  112.6 39.7 all-gather.17
  154.0 37.8 all-gather.13
  193.6 37.8 all-gather.21
  234.2 58.4 all-gather.19
  294.5 40.6 all-gather.25
  338.2 54.2 all-gather.23
  394.3 39.7 all-gather.27
